TPU v7x, 32 devices: a whole 2x2x4 slice. The times are simulated.
32 devices in a mesh: groups: 2 (over x), space: 8 (over z, y), beam: 2 (over core).
Axes of the slice: x: 2, y: 2, z: 4, core: 2. Of those that a mesh axis runs over, the one named last changes fastest.
Arguments:
- s_matrix: bfloat16 [4096, 256, 480], P(('groups', 'beam'), 'space'), parts along dimension 0, may hold values from -6 to 6
- beam_index: int32 [2048, 2], P('beam'), may hold values from -24 to 23, as said below
- beam_amp: float32 [2048], P('beam'), may hold values from 0.5 to 2
- beam_phase: float32 [2048], P('beam'), may hold values from -3.140625 to 3.140625
- positions: int32 [2, 384, 2], replicated, may hold values from 0 to 239
Outputs:
- intensities: float32 [4, 384, 256, 240], P('groups', ('space', 'beam')), parts along dimension 0
There are 2 independent parts, one for each index of `groups`. A program takes and returns all parts, laid end to end along the dimension named above; an argument that names none is the same for every part. Nothing has to cross between parts.
Inputs may be any that keep to these rules, and one draw needn't show every extreme that they name: `beam_index`: no two beams have the same wave-vector.
All inputs are finite; a program needn't handle non-finite values.
Results may differ from a plain program's by a relative error of at most 0.0072.
Values may be sent and summed in bfloat16 or wider, within the bound.
No kernel may reach another device: no remote copies, remote signals or barrier semaphores. Data moves between devices by JAX's collectives and lax.ppermute only.
A program may use at most 192 MiB of HBM per device.

v0:
```python
import math
import jax
import jax.numpy as jnp
from jax import lax
from jax.sharding import PartitionSpec as P

NB = 2048
RY = 256
RX = 240


def dft_tables():
    xs = jnp.arange(RX, dtype=jnp.int32)
    prod_x = jnp.mod(xs[:, None] * xs[None, :], RX).astype(jnp.float32)
    angle_x = 2.0 * math.pi / RX * prod_x
    cos_x = jnp.cos(angle_x) / math.sqrt(RX)
    sin_x = jnp.sin(angle_x) / math.sqrt(RX)
    table_x = jnp.concatenate(
        [jnp.concatenate([cos_x, -sin_x], 1), jnp.concatenate([sin_x, cos_x], 1)], 0
    ).astype(jnp.bfloat16)
    ys = jnp.arange(RY, dtype=jnp.int32)
    prod_y = jnp.mod(ys[:, None] * ys[None, :], RY).astype(jnp.float32)
    angle_y = 2.0 * math.pi / RY * prod_y
    table_y = jnp.concatenate([jnp.cos(angle_y), jnp.sin(angle_y)], 0) / math.sqrt(RY)
    return (table_x, table_y.astype(jnp.bfloat16))


def coefficients(spots, beam_index, beam_amp, beam_phase):
    rows_part = jnp.mod(spots[:, 0:1] * beam_index[None, :, 0], RY).astype(jnp.float32)
    cols_part = jnp.mod(spots[:, 1:2] * beam_index[None, :, 1], RX).astype(jnp.float32)
    theta = beam_phase[None, :] - 2.0 * math.pi * (rows_part / RY + cols_part / RX)
    scale = beam_amp[None, :] / math.sqrt(NB)
    return (
        (scale * jnp.cos(theta)).astype(jnp.bfloat16),
        (scale * jnp.sin(theta)).astype(jnp.bfloat16),
    )


def body(s_matrix, beam_index, beam_amp, beam_phase, positions):
    local_beams = s_matrix.shape[0]
    local_rows = s_matrix.shape[1]
    n_space = lax.axis_size("space")
    n_beam = lax.axis_size("beam")
    n_batch = positions.shape[0]
    per_device = positions.shape[1] // (n_space * n_beam)
    flat_s = s_matrix.reshape(local_beams, local_rows * 2 * RX)
    table_x, table_y = dft_tables()

    def transform(wave, count):
        half = jnp.dot(wave.reshape(-1, 2 * RX), table_x, preferred_element_type=jnp.float32)
        half = half.astype(jnp.bfloat16).reshape(-1, RY, 2 * RX)
        spectrum = jnp.einsum("vy,pyc->pvc", table_y, half, preferred_element_type=jnp.float32)
        spec_re = spectrum[:, :RY, :RX] + spectrum[:, RY:, RX:]
        spec_im = spectrum[:, :RY, RX:] - spectrum[:, RY:, :RX]
        return (spec_re * spec_re + spec_im * spec_im).reshape(count, per_device, RY, RX)

    def one_group(chosen):
        count = chosen.shape[0]
        blocks = chosen.reshape(count, n_space, n_beam, per_device, 2)
        spots = jnp.transpose(blocks, (2, 1, 0, 3, 4)).reshape(-1, 2)
        coef_re, coef_im = coefficients(spots, beam_index, beam_amp, beam_phase)
        total_rows = spots.shape[0]
        product = jnp.dot(
            jnp.concatenate([coef_re, coef_im], 0), flat_s, preferred_element_type=jnp.float32
        )
        product = product.reshape(
            2, total_rows // n_beam * lax.axis_size("beam"), local_rows, 2 * RX
        )
        wave_re = product[0, ..., :RX] - product[1, ..., RX:]
        wave_im = product[0, ..., RX:] + product[1, ..., :RX]
        rounded = lax.optimization_barrier(
            jnp.concatenate([wave_re, wave_im], -1).astype(jnp.bfloat16)
        )
        summed = lax.psum_scatter(
            rounded.astype(jnp.float32).astype(jnp.bfloat16),
            "beam",
            scatter_dimension=0,
            tiled=True,
        )
        wave = lax.all_to_all(summed, "space", split_axis=0, concat_axis=1, tiled=True)
        return transform(wave, count)

    outputs = [one_group(positions[batch : batch + 1]) for batch in range(n_batch)]
    return jnp.concatenate(outputs, 0)


def solution(mesh):
    in_specs = (P(("groups", "beam"), "space", None), P("beam", None), P("beam"), P("beam"), P())
    out_specs = P("groups", ("space", "beam"), None, None)
    return jax.shard_map(body, mesh=mesh, in_specs=in_specs, out_specs=out_specs, check_vma=False)
```

profile of v0, /device:TPU:0, one launch (start us, length us, event | category | flops | bytes accessed | tf_op | source)
XLA Modules:
  0.0 513.1 jit_solution(4622857411658525311)
XLA Ops:
  6.5 0.7 broadcast_multiply_fusion
  7.2 0.7 fusion.71
  7.9 0.8 fusion.70
  9.2 16.0 %multiply_convert_fusion.3 = (bf16[384,1024]{1,0:T(8,128)(2,1)S(1)}, bf16[384,1024]{1,0:T(8,128)(2,1)S(1)}, bf16[384,1024]{1,0:T(8,128)(2,1)S(1)}, bf16[384,1024]{1,0:T(8,128)(2,1)S(1)}) fusion(s32[1024]{0:T(1024)S(1)} %bitcast.92, s32[384]{0:T(512)S(1)} %get-tuple-element.6, s32[1024]{0:T(1024)S(1)} %bitcast.91, s32[384]{0:T(512)S(1)} %get-tuple-element.5, ...), kind=kLoop, calls=%fused_computation.75 | loop fusion | flops 23592960 | bytes 3168256 | tf_op jit(solution)/shard_map/convert_element_type | solution.py:34
  25.2 1.5 pad_maximum_fusion.3
  26.7 34.1 %fusion = f32[2,384,32,480]{1,3,2,0:T(8,128)} fusion(bf16[2,384,1024,1]{2,1,3,0:T(8,128)(2,1)S(1)} %bitcast.88, bf16[1024,32,480]{0,2,1:T(8,128)(2,1)} %param.5), kind=kOutput, calls=%fused_computation | convolution fusion | flops 24159191040 | bytes 80216064 | tf_op jit(solution)/shard_map/dot_general | solution.py:63
  60.7 15.8 %fusion.10 = (bf16[384,32,240]{0,2,1:T(8,128)(2,1)S(1)}, bf16[384,32,240]{0,2,1:T(8,128)(2,1)S(1)}) fusion(f32[2,384,32,480]{1,3,2,0:T(8,128)} %fusion), kind=kLoop, calls=%fused_computation.21 | loop fusion | flops 11796480 | bytes 58982400 | tf_op jit(solution)/shard_map/sub | solution.py:69
  76.6 5.5 %pad_maximum_fusion.1 = bf16[384,32,480]{0,2,1:T(8,128)(2,1)} fusion(bf16[384,32,240]{0,2,1:T(8,128)(2,1)S(1)} %get-tuple-element.12, bf16[384,32,240]{0,2,1:T(8,128)(2,1)S(1)} %get-tuple-element.11), kind=kLoop, calls=%fused_computation.13 | loop fusion | flops 23592960 | bytes 23592960 | tf_op jit(solution)/shard_map/concatenate | solution.py:72
  82.1 16.8 %copy.21 = bf16[384,32,480]{2,1,0:T(8,128)(2,1)} copy(bf16[384,32,480]{0,2,1:T(8,128)(2,1)} %pad_maximum_fusion.1) | data formatting | bytes 23592960 | tf_op jit(solution)/shard_map/optimization_barrier | solution.py:71
  98.8 0.2 reduce-scatter.3.cloned.1.call-start
  99.1 1.2 copy-done
  100.2 35.8 %fusion.2 = f32[2,384,32,480]{1,3,2,0:T(8,128)} fusion(bf16[2,384,1024,1]{2,1,3,0:T(8,128)(2,1)S(1)} %bitcast.87, bf16[1024,32,480]{0,2,1:T(8,128)(2,1)} %param.5), kind=kOutput, calls=%fused_computation.2 | convolution fusion | flops 24159191040 | bytes 80216064 | tf_op jit(solution)/shard_map/dot_general | solution.py:63
  136.0 15.8 %fusion.8 = (bf16[384,32,240]{0,2,1:T(8,128)(2,1)S(1)}, bf16[384,32,240]{0,2,1:T(8,128)(2,1)S(1)}) fusion(f32[2,384,32,480]{1,3,2,0:T(8,128)} %fusion.2), kind=kLoop, calls=%fused_computation.19 | loop fusion | flops 11796480 | bytes 58982400 | tf_op jit(solution)/shard_map/sub | solution.py:69
  151.8 5.5 %pad_maximum_fusion = bf16[384,32,480]{0,2,1:T(8,128)(2,1)} fusion(bf16[384,32,240]{0,2,1:T(8,128)(2,1)S(1)} %get-tuple-element.10, bf16[384,32,240]{0,2,1:T(8,128)(2,1)S(1)} %get-tuple-element.9), kind=kLoop, calls=%fused_computation.12 | loop fusion | flops 23592960 | bytes 23592960 | tf_op jit(solution)/shard_map/concatenate | solution.py:72
  157.3 16.6 %copy.17 = bf16[384,32,480]{2,1,0:T(8,128)(2,1)} copy(bf16[384,32,480]{0,2,1:T(8,128)(2,1)} %pad_maximum_fusion) | data formatting | bytes 23592960 | tf_op jit(solution)/shard_map/optimization_barrier | solution.py:71
  174.0 7.6 %all-to-all-start.1 = ((bf16[192,32,480]{2,1,0:T(8,128)(2,1)}), bf16[192,32,480]{2,1,0:T(8,128)(2,1)}, u32[]{:S(2)}, u32[]{:S(2)}) async-start(bf16[192,32,480]{2,1,0:T(8,128)(2,1)} %reduce-scatter.5.cloned.1.call-done), calls=%async_computation.3 | async-start | bytes 12582912 | tf_op jit(solution)/shard_map/all_to_all | solution.py:80
  181.6 16.3 %reduce-scatter.3.cloned.1.call-done = bf16[192,32,480]{2,1,0:T(8,128)(2,1)} async-done(((bf16[384,32,480]{2,1,0:T(8,128)(2,1)}), bf16[192,32,480]{2,1,0:T(8,128)(2,1)}) %reduce-scatter.3.cloned.1.call-update) | async-done | bytes 5898256 | tf_op jit(solution)/shard_map/reduce_scatter | solution.py:74
  197.9 121.8 %all-to-all-done.1 = bf16[192,32,480]{2,1,0:T(8,128)(2,1)} async-done(((bf16[192,32,480]{2,1,0:T(8,128)(2,1)}), bf16[192,32,480]{2,1,0:T(8,128)(2,1)}, u32[]{:S(2)}, u32[]{:S(2)}) %all-to-all-start.1) | async-done | bytes 5898272 | tf_op jit(solution)/shard_map/all_to_all | solution.py:80
  319.7 5.0 all-to-all-start
  324.7 1.0 fusion.59
  325.6 1.1 negate_convert_fusion
  326.7 1.0 fusion.60
  327.8 3.4 copy.22
  331.2 4.0 convolution_convert_fusion
  335.2 9.6 %convolution_bitcast_fusion = f32[24,512,480]{1,2,0:T(8,128)} fusion(bf16[60,24,8,256]{3,2,1,0:T(8,128)(2,1)S(1)} %bitcast.82, f32[256,256]{1,0:T(8,128)S(1)} %get-tuple-element.27, f32[256,256]{1,0:T(8,128)S(1)} %get-tuple-element.28), kind=kOutput, calls=%fused_computation.17 | convolution fusion | flops 3020292096 | bytes 30015488 | tf_op jit(solution)/shard_map/vy,pyc->pvc/dot_general | solution.py:52
  344.8 11.4 %fusion.18 = f32[1,24,256,240]{2,3,1,0:T(8,128)} fusion(f32[24,512,480]{1,2,0:T(8,128)} %convolution_bitcast_fusion), kind=kLoop, calls=%fused_computation.30 | loop fusion | flops 7372800 | bytes 29491200 | tf_op jit(solution)/shard_map/reshape | solution.py:55
  356.2 105.5 %all-to-all-done = bf16[192,32,480]{2,1,0:T(8,128)(2,1)} async-done(((bf16[192,32,480]{2,1,0:T(8,128)(2,1)}), bf16[192,32,480]{2,1,0:T(8,128)(2,1)}, u32[]{:S(2)}, u32[]{:S(2)}) %all-to-all-start) | async-done | bytes 5898272 | tf_op jit(solution)/shard_map/all_to_all | solution.py:80
  461.7 6.6 %copy.18 = bf16[24,8,32,480]{3,2,1,0:T(8,128)(2,1)} copy(bf16[24,8,32,480]{3,2,0,1:T(8,128)(2,1)} %bitcast.13) | data formatting | bytes 11796480 | tf_op jit(solution)/shard_map/all_to_all | solution.py:80
  468.3 8.7 %convolution_convert_fusion.1 = bf16[6144,480]{0,1:T(8,128)(2,1)S(1)} fusion(bf16[6144,480]{1,0:T(8,128)(2,1)} %bitcast.85, bf16[240,240]{1,0:T(8,128)(2,1)S(1)} %get-tuple-element.26, bf16[240,240]{1,0:T(8,128)(2,1)S(1)} %fusion.59, bf16[240,240]{1,0:T(8,128)(2,1)S(1)} %get-tuple-element.25), kind=kOutput, calls=%fused_computation.16 | convolution fusion | flops 2835947520 | bytes 12142080 | tf_op jit(solution)/shard_map/dot_general | solution.py:50
  477.0 9.9 %convolution_bitcast_fusion.1 = f32[24,512,480]{1,2,0:T(8,128)} fusion(bf16[60,24,8,256]{3,2,1,0:T(8,128)(2,1)S(1)} %bitcast.81, f32[256,256]{1,0:T(8,128)S(1)} %get-tuple-element.27, f32[256,256]{1,0:T(8,128)S(1)} %get-tuple-element.28), kind=kOutput, calls=%fused_computation.18 | convolution fusion | flops 3020292096 | bytes 30015488 | tf_op jit(solution)/shard_map/vy,pyc->pvc/dot_general | solution.py:52
  486.9 11.4 %fusion.22 = f32[1,24,256,240]{2,3,1,0:T(8,128)} fusion(f32[24,512,480]{1,2,0:T(8,128)} %convolution_bitcast_fusion.1), kind=kLoop, calls=%fused_computation.36 | loop fusion | flops 7372800 | bytes 29491200 | tf_op jit(solution)/shard_map/reshape | solution.py:55
  498.3 8.0 %pad_maximum_fusion.2 = f32[2,24,256,240]{2,3,1,0:T(8,128)} fusion(f32[1,24,256,240]{2,3,1,0:T(8,128)S(1)} %bitcast.84, f32[1,24,256,240]{2,3,1,0:T(8,128)} %fusion.22), kind=kLoop, calls=%fused_computation.14 | loop fusion | flops 2949120 | bytes 23592960 | tf_op jit(solution)/shard_map/concatenate | solution.py:84
  (18 shorter events, 0.5 us)
Async XLA Ops:
  6.5 167.5 %reduce-scatter.5.cloned.1.call-start = ((), (), s32[]{:S(2)}) async-start(), calls=%async_computation.5 | async-start | bytes 18874368 | tf_op jit(solution)/shard_map/reduce_scatter | solution.py:74
  98.8 1.4 copy-start
  98.8 99.1 %reduce-scatter.3.cloned.1.call-start = ((), (), s32[]{:S(2)}) async-start(), calls=%async_computation.4 | async-start | bytes 18874368 | tf_op jit(solution)/shard_map/reduce_scatter | solution.py:74
  174.0 145.7 %all-to-all-start.1 = ((bf16[192,32,480]{2,1,0:T(8,128)(2,1)}), bf16[192,32,480]{2,1,0:T(8,128)(2,1)}, u32[]{:S(2)}, u32[]{:S(2)}) async-start(bf16[192,32,480]{2,1,0:T(8,128)(2,1)} %reduce-scatter.5.cloned.1.call-done), calls=%async_computation.3 | async-start | bytes 12582912 | tf_op jit(solution)/shard_map/all_to_all | solution.py:80
  319.7 142.1 %all-to-all-start = ((bf16[192,32,480]{2,1,0:T(8,128)(2,1)}), bf16[192,32,480]{2,1,0:T(8,128)(2,1)}, u32[]{:S(2)}, u32[]{:S(2)}) async-start(bf16[192,32,480]{2,1,0:T(8,128)(2,1)} %reduce-scatter.3.cloned.1.call-done), calls=%async_computation.1 | async-start | bytes 12582912 | tf_op jit(solution)/shard_map/all_to_all | solution.py:80
  468.3 29.9 %slice-start = ((s8[5898240]{0:T(1024)(128)(4,1)}), s8[4194304]{0:T(1024)(128)(4,1)S(1)}, s32[]{:S(2)}) async-start(s8[5898240]{0:T(1024)(128)(4,1)} %bitcast.83), calls=%async_computation.6 | async-start | bytes 8388608
  477.0 21.3 %slice-start.1 = ((s8[5898240]{0:T(1024)(128)(4,1)}), s8[1703936]{0:T(1024)(128)(4,1)S(1)}, s32[]{:S(2)}) async-start(s8[5898240]{0:T(1024)(128)(4,1)} %bitcast.83), calls=%async_computation.7 | async-start | bytes 3407872
Sparse Core Ops, SparseCore 0:
  99.0 23.4 reduce-scatter.4
  174.1 23.7 reduce-scatter.2
where the time goes:
time: 515 us; the launch traced here: 513 us
  waiting for transfers between devices  244 us (47%)
  matrix products  102 us (20%)
  other arithmetic  94.6 us (18%)
  local copies, waits for them, and re-layouts  46.4 us (9%)
  between operations  13.6 us (3%)
  starting transfers between devices  12.8 us (2%)
    all_to_all x2, waiting for transfers between devices, one_group(): lax.all_to_all(summed, 'space', split_axis=0, concat_axis=1, tiled=True)  227 us
    dot_general x2, matrix products, one_group(): jnp.dot(jnp.concatenate([coef_re, coef_im], 0), flat_s, preferred_element...  69.8 us
    optimization_barrier x2, local copies, waits for them, and re-layouts, one_group(): lax.optimization_barrier(jnp.concatenate([wave_re, wave_im], -1).astype(j...  33.4 us
    sub x2, other arithmetic, one_group(): wave_re = product[0, ..., :RX] - product[1, ..., RX:]  31.6 us
    reshape x2, other arithmetic, transform(): (spec_re * spec_re + spec_im * spec_im).reshape(count, per_device, RY, RX)  22.7 us
    dot_general x2, matrix products, transform(): jnp.einsum('vy,pyc->pvc', table_y, half, preferred_element_type=jnp.float32)  19.5 us
    reduce_scatter x2, waiting for transfers between devices, one_group(): lax.psum_scatter(rounded.astype(jnp.float32).astype(jnp.bfloat16), 'beam'...  16.3 us
    convert_element_type x1, other arithmetic, coefficients(): (scale * jnp.cos(theta)).astype(jnp.bfloat16)  16 us
  transfers between devices with their start and end apart: 4, of which 3 were waited for; matrix products, arithmetic and copies ran while one was open for 21% of the time, Pallas kernels for 0%

commit v1 on v0

--- a/solution.py
+++ b/solution.py
@@ -7,6 +7,12 @@
 NB = 2048
 RY = 256
 RX = 240
+
+
+def exchange_blocks(value, mesh_axis, split, join):
+    cells = jnp.split(value, lax.axis_size(mesh_axis), axis=split)
+    got = lax.all_to_all(jnp.stack(cells), mesh_axis, 0, 0)
+    return jnp.concatenate(got, axis=join)
 
 
 def dft_tables():
@@ -77,7 +83,7 @@
             scatter_dimension=0,
             tiled=True,
         )
-        wave = lax.all_to_all(summed, "space", split_axis=0, concat_axis=1, tiled=True)
+        wave = exchange_blocks(summed, "space", 0, 1)
         return transform(wave, count)
 
     outputs = [one_group(positions[batch : batch + 1]) for batch in range(n_batch)]

time: 515 us -> 533 us (1.035)
  local copies, waits for them, and re-layouts: 46.4 us -> 80.7 us
  waiting for transfers between devices: 244 us -> 227 us
    unnamed x6 -> x20, local copies, waits for them, and re-layouts: 1.16 us -> 31 us
    reduce_scatter x2, waiting for transfers between devices: 16.3 us -> 0.03 us  [one_group(): lax.psum_scatter(rounded.astype(jnp.float32).astype(jnp.bfloat16), 'beam'...]
    all_to_all x2 -> x0, local copies, waits for them, and re-layouts: 10 us -> none  [one_group(): lax.all_to_all(summed, 'space', split_axis=0, concat_axis=1, tiled=True)]
    reshape x0 -> x2, local copies, waits for them, and re-layouts: none -> 10 us  [exchange_blocks(): return jnp.concatenate(got, axis=join)]
  transfers between devices with their start and end apart: 4 -> 4, of which waited for: 3 -> 2; matrix products, arithmetic and copies ran while one was open for 21% -> 26% of each run, Pallas kernels for 0% -> 0%
where the time goes in v1:
time: 533 us; the launch traced here: 531 us
  waiting for transfers between devices  227 us (43%)
  matrix products  102 us (19%)
  other arithmetic  94.6 us (18%)
  local copies, waits for them, and re-layouts  80.7 us (15%)
  between operations  13.6 us (3%)
  starting transfers between devices  13 us (2%)
    all_to_all x2, waiting for transfers between devices, exchange_blocks(): got = lax.all_to_all(jnp.stack(cells), mesh_axis, 0, 0)  227 us
    dot_general x2, matrix products, one_group(): jnp.dot(jnp.concatenate([coef_re, coef_im], 0), flat_s, preferred_element...  69.8 us
    optimization_barrier x2, local copies, waits for them, and re-layouts, one_group(): lax.optimization_barrier(jnp.concatenate([wave_re, wave_im], -1).astype(j...  33.4 us
    sub x2, other arithmetic, one_group(): wave_re = product[0, ..., :RX] - product[1, ..., RX:]  31.6 us
    unnamed x20, local copies, waits for them, and re-layouts  31 us
    reshape x2, other arithmetic, transform(): (spec_re * spec_re + spec_im * spec_im).reshape(count, per_device, RY, RX)  22.7 us
    dot_general x2, matrix products, transform(): jnp.einsum('vy,pyc->pvc', table_y, half, preferred_element_type=jnp.float32)  19.5 us
    convert_element_type x1, other arithmetic, coefficients(): (scale * jnp.cos(theta)).astype(jnp.bfloat16)  16 us
  transfers between devices with their start and end apart: 4, of which 2 were waited for; matrix products, arithmetic and copies ran while one was open for 26% of the time, Pallas kernels for 0%

profile of v1, /device:TPU:0, one launch (start us, length us, event | category | flops | bytes accessed | tf_op | source)
XLA Modules:
  0.0 530.7 jit_solution(6259875964393075119)
XLA Ops:
  9.2 16.0 %multiply_convert_fusion.3 = (bf16[384,1024]{1,0:T(8,128)(2,1)S(1)}, bf16[384,1024]{1,0:T(8,128)(2,1)S(1)}, bf16[384,1024]{1,0:T(8,128)(2,1)S(1)}, bf16[384,1024]{1,0:T(8,128)(2,1)S(1)}) fusion(s32[1024]{0:T(1024)S(1)} %bitcast.152, s32[384]{0:T(512)S(1)} %get-tuple-element.6, s32[1024]{0:T(1024)S(1)} %bitcast.151, s32[384]{0:T(512)S(1)} %get-tuple-element.5, ...), kind=kLoop, calls=%fused_computation.75 | loop fusion | flops 23592960 | bytes 3168256 | tf_op jit(solution)/shard_map/convert_element_type | solution.py:40
  26.7 34.1 %fusion = f32[2,384,32,480]{1,3,2,0:T(8,128)} fusion(bf16[2,384,1024,1]{2,1,3,0:T(8,128)(2,1)S(1)} %bitcast.148, bf16[1024,32,480]{0,2,1:T(8,128)(2,1)} %param.5), kind=kOutput, calls=%fused_computation | convolution fusion | flops 24159191040 | bytes 80216064 | tf_op jit(solution)/shard_map/dot_general | solution.py:69
  60.7 15.8 %fusion.10 = (bf16[384,32,240]{0,2,1:T(8,128)(2,1)S(1)}, bf16[384,32,240]{0,2,1:T(8,128)(2,1)S(1)}) fusion(f32[2,384,32,480]{1,3,2,0:T(8,128)} %fusion), kind=kLoop, calls=%fused_computation.21 | loop fusion | flops 11796480 | bytes 58982400 | tf_op jit(solution)/shard_map/sub | solution.py:75
  76.6 5.5 %pad_maximum_fusion.1 = bf16[384,32,480]{0,2,1:T(8,128)(2,1)} fusion(bf16[384,32,240]{0,2,1:T(8,128)(2,1)S(1)} %get-tuple-element.12, bf16[384,32,240]{0,2,1:T(8,128)(2,1)S(1)} %get-tuple-element.11), kind=kLoop, calls=%fused_computation.13 | loop fusion | flops 23592960 | bytes 23592960 | tf_op jit(solution)/shard_map/concatenate | solution.py:78
  82.1 16.8 %copy.19 = bf16[384,32,480]{2,1,0:T(8,128)(2,1)} copy(bf16[384,32,480]{0,2,1:T(8,128)(2,1)} %pad_maximum_fusion.1) | data formatting | bytes 23592960 | tf_op jit(solution)/shard_map/optimization_barrier | solution.py:77
  100.2 35.8 %fusion.2 = f32[2,384,32,480]{1,3,2,0:T(8,128)} fusion(bf16[2,384,1024,1]{2,1,3,0:T(8,128)(2,1)S(1)} %bitcast.147, bf16[1024,32,480]{0,2,1:T(8,128)(2,1)} %param.5), kind=kOutput, calls=%fused_computation.2 | convolution fusion | flops 24159191040 | bytes 80216064 | tf_op jit(solution)/shard_map/dot_general | solution.py:69
  136.0 15.8 %fusion.8 = (bf16[384,32,240]{0,2,1:T(8,128)(2,1)S(1)}, bf16[384,32,240]{0,2,1:T(8,128)(2,1)S(1)}) fusion(f32[2,384,32,480]{1,3,2,0:T(8,128)} %fusion.2), kind=kLoop, calls=%fused_computation.19 | loop fusion | flops 11796480 | bytes 58982400 | tf_op jit(solution)/shard_map/sub | solution.py:75
  151.8 5.5 %pad_maximum_fusion = bf16[384,32,480]{0,2,1:T(8,128)(2,1)} fusion(bf16[384,32,240]{0,2,1:T(8,128)(2,1)S(1)} %get-tuple-element.10, bf16[384,32,240]{0,2,1:T(8,128)(2,1)S(1)} %get-tuple-element.9), kind=kLoop, calls=%fused_computation.12 | loop fusion | flops 23592960 | bytes 23592960 | tf_op jit(solution)/shard_map/concatenate | solution.py:78
  157.3 16.6 %copy.15 = bf16[384,32,480]{2,1,0:T(8,128)(2,1)} copy(bf16[384,32,480]{0,2,1:T(8,128)(2,1)} %pad_maximum_fusion) | data formatting | bytes 23592960 | tf_op jit(solution)/shard_map/optimization_barrier | solution.py:77
  174.0 2.1 fusion.53
  182.4 2.3 fusion.49
  186.8 2.4 fusion.47
  189.1 2.4 fusion.46
  191.5 7.9 %all-to-all-start.1 = ((bf16[8,24,32,480]{3,2,1,0:T(8,128)(2,1)}), bf16[8,24,32,480]{3,2,1,0:T(8,128)(2,1)}, u32[]{:S(2)}, u32[]{:S(2)}) async-start(bf16[8,24,32,480]{3,2,1,0:T(8,128)(2,1)} %fusion.46), calls=%async_computation.3 | async-start | bytes 12582912 | tf_op jit(solution)/shard_map/all_to_all | solution.py:14
  199.4 2.1 fusion.61
  201.5 2.1 fusion.60
  207.8 2.1 fusion.57
  209.9 2.1 fusion.56
  212.0 2.1 fusion.55
  214.1 2.1 fusion.54
  216.2 121.0 %all-to-all-done.1 = bf16[8,24,32,480]{3,2,1,0:T(8,128)(2,1)} async-done(((bf16[8,24,32,480]{3,2,1,0:T(8,128)(2,1)}), bf16[8,24,32,480]{3,2,1,0:T(8,128)(2,1)}, u32[]{:S(2)}, u32[]{:S(2)}) %all-to-all-start.1) | async-done | bytes 5898272 | tf_op jit(solution)/shard_map/all_to_all | solution.py:14
  337.2 5.0 all-to-all-start
  345.2 3.4 copy.20
  348.6 4.0 convolution_convert_fusion
  352.7 9.6 %convolution_bitcast_fusion = f32[24,512,480]{1,2,0:T(8,128)} fusion(bf16[60,24,8,256]{3,2,1,0:T(8,128)(2,1)S(1)} %bitcast.142, f32[256,256]{1,0:T(8,128)S(1)} %get-tuple-element.27, f32[256,256]{1,0:T(8,128)S(1)} %get-tuple-element.28), kind=kOutput, calls=%fused_computation.17 | convolution fusion | flops 3020292096 | bytes 30015488 | tf_op jit(solution)/shard_map/vy,pyc->pvc/dot_general | solution.py:58
  362.3 11.4 %fusion.18 = f32[1,24,256,240]{2,3,1,0:T(8,128)} fusion(f32[24,512,480]{1,2,0:T(8,128)} %convolution_bitcast_fusion), kind=kLoop, calls=%fused_computation.30 | loop fusion | flops 7372800 | bytes 29491200 | tf_op jit(solution)/shard_map/reshape | solution.py:61
  373.7 105.7 %all-to-all-done = bf16[8,24,32,480]{3,2,1,0:T(8,128)(2,1)} async-done(((bf16[8,24,32,480]{3,2,1,0:T(8,128)(2,1)}), bf16[8,24,32,480]{3,2,1,0:T(8,128)(2,1)}, u32[]{:S(2)}, u32[]{:S(2)}) %all-to-all-start) | async-done | bytes 5898272 | tf_op jit(solution)/shard_map/all_to_all | solution.py:14
  479.3 6.6 %copy.16 = bf16[24,8,32,480]{3,2,1,0:T(8,128)(2,1)} copy(bf16[24,8,32,480]{3,2,0,1:T(8,128)(2,1)} %bitcast.20) | data formatting | bytes 11796480 | tf_op jit(solution)/shard_map/reshape | solution.py:15
  485.9 8.7 %convolution_convert_fusion.1 = bf16[6144,480]{0,1:T(8,128)(2,1)S(1)} fusion(bf16[6144,480]{1,0:T(8,128)(2,1)} %bitcast.145, bf16[240,240]{1,0:T(8,128)(2,1)S(1)} %get-tuple-element.26, bf16[240,240]{1,0:T(8,128)(2,1)S(1)} %fusion.75, bf16[240,240]{1,0:T(8,128)(2,1)S(1)} %get-tuple-element.25), kind=kOutput, calls=%fused_computation.16 | convolution fusion | flops 2835947520 | bytes 12142080 | tf_op jit(solution)/shard_map/dot_general | solution.py:56
  494.6 9.9 %convolution_bitcast_fusion.1 = f32[24,512,480]{1,2,0:T(8,128)} fusion(bf16[60,24,8,256]{3,2,1,0:T(8,128)(2,1)S(1)} %bitcast.141, f32[256,256]{1,0:T(8,128)S(1)} %get-tuple-element.27, f32[256,256]{1,0:T(8,128)S(1)} %get-tuple-element.28), kind=kOutput, calls=%fused_computation.18 | convolution fusion | flops 3020292096 | bytes 30015488 | tf_op jit(solution)/shard_map/vy,pyc->pvc/dot_general | solution.py:58
  504.5 11.4 %fusion.22 = f32[1,24,256,240]{2,3,1,0:T(8,128)} fusion(f32[24,512,480]{1,2,0:T(8,128)} %convolution_bitcast_fusion.1), kind=kLoop, calls=%fused_computation.36 | loop fusion | flops 7372800 | bytes 29491200 | tf_op jit(solution)/shard_map/reshape | solution.py:61
  515.9 8.0 %pad_maximum_fusion.2 = f32[2,24,256,240]{2,3,1,0:T(8,128)} fusion(f32[1,24,256,240]{2,3,1,0:T(8,128)S(1)} %bitcast.144, f32[1,24,256,240]{2,3,1,0:T(8,128)} %fusion.22), kind=kLoop, calls=%fused_computation.14 | loop fusion | flops 2949120 | bytes 23592960 | tf_op jit(solution)/shard_map/concatenate | solution.py:90
  (34 shorter events, 21.1 us)
Async XLA Ops:
  6.5 167.5 %reduce-scatter.5.cloned.1.call-start = ((), (), s32[]{:S(2)}) async-start(), calls=%async_computation.5 | async-start | bytes 18874368 | tf_op jit(solution)/shard_map/reduce_scatter | solution.py:80
  98.8 1.4 copy-start
  98.8 100.5 %reduce-scatter.3.cloned.1.call-start = ((), (), s32[]{:S(2)}) async-start(), calls=%async_computation.4 | async-start | bytes 18874368 | tf_op jit(solution)/shard_map/reduce_scatter | solution.py:80
  191.5 145.7 %all-to-all-start.1 = ((bf16[8,24,32,480]{3,2,1,0:T(8,128)(2,1)}), bf16[8,24,32,480]{3,2,1,0:T(8,128)(2,1)}, u32[]{:S(2)}, u32[]{:S(2)}) async-start(bf16[8,24,32,480]{3,2,1,0:T(8,128)(2,1)} %fusion.46), calls=%async_computation.3 | async-start | bytes 12582912 | tf_op jit(solution)/shard_map/all_to_all | solution.py:14
  337.2 142.1 %all-to-all-start = ((bf16[8,24,32,480]{3,2,1,0:T(8,128)(2,1)}), bf16[8,24,32,480]{3,2,1,0:T(8,128)(2,1)}, u32[]{:S(2)}, u32[]{:S(2)}) async-start(bf16[8,24,32,480]{3,2,1,0:T(8,128)(2,1)} %fusion.54), calls=%async_computation.1 | async-start | bytes 12582912 | tf_op jit(solution)/shard_map/all_to_all | solution.py:14
  485.9 29.9 %slice-start = ((s8[5898240]{0:T(1024)(128)(4,1)}), s8[4194304]{0:T(1024)(128)(4,1)S(1)}, s32[]{:S(2)}) async-start(s8[5898240]{0:T(1024)(128)(4,1)} %bitcast.143), calls=%async_computation.6 | async-start | bytes 8388608
  494.6 21.3 %slice-start.1 = ((s8[5898240]{0:T(1024)(128)(4,1)}), s8[1703936]{0:T(1024)(128)(4,1)S(1)}, s32[]{:S(2)}) async-start(s8[5898240]{0:T(1024)(128)(4,1)} %bitcast.143), calls=%async_computation.7 | async-start | bytes 3407872
Sparse Core Ops, SparseCore 0:
  99.0 23.4 reduce-scatter.4
  174.1 23.7 reduce-scatter.2
